TPU v7x, 256 devices: a whole 4x4x8 slice. The times are simulated.
256 devices in a mesh: grp: 4 (over z_lo), row: 4 (over x), col: 16 (over y, z_hi, core).
Axes of the slice: x: 4, y: 4, z: 8 (z_hi: 2, z_lo: 4; z = z_hi * 4 + z_lo), core: 2. Of those that a mesh axis runs over, the one named last changes fastest.
Arguments:
- outer_params: float32 [8192, 1024], P('col', 'row'), may hold values from -0.0625 to 0.0625
- first_moment: float32 [4, 8192, 1024], P('grp', 'col', 'row'), may hold values from -0.12 to 0.12
- second_moment: float32 [4, 8192, 1024], P('grp', 'col', 'row'), may hold values from 0.0001 to 0.01
- outer_moment: float32 [8192, 1024], P('col', 'row'), may hold values from -0.06 to 0.06
- activations: bfloat16 [4, 3, 2048, 8192], P('grp', None, 'row', 'col'), may hold values from -6 to 6
- targets: bfloat16 [4, 3, 2048, 1024], P('grp', None, 'col', 'row'), may hold values from -6 to 6
Outputs:
- new_params: float32 [8192, 1024], P('col', 'row')
- new_moment: float32 [8192, 1024], P('col', 'row')
All inputs are finite; a program needn't handle non-finite values.
Results may differ from a plain program's by a relative error of at most 0.0054.
Values may be sent and summed in bfloat16 or wider, within the bound.
A program may use at most 64 MiB of HBM per device.

v0:
```python
import jax
import jax.numpy as jnp
from jax import lax
from jax.sharding import Mesh
from jax.sharding import PartitionSpec as P

TOKENS = 2048
STEPS = 3
SLOW_STEPS = 1
PRIOR = 100
COL = ("col_0", "col_1", "col_2")
beta_first = 0.9
beta_second = 0.95
inner_rate = 0.01
decay_rate = 0.1
epsilon_value = 1e-08
outer_rate = 0.7
momentum_coef = 0.9


def split_up(shard, dim, count):
    before, after = (shard.shape[:dim], shard.shape[dim + 1 :])
    return jnp.moveaxis(shard.reshape(*before, count, -1, *after), dim, 0)


def summed_on_arrival(shard, axis, dim):
    count = lax.axis_size(axis)
    parts = lax.all_to_all(split_up(shard, dim, count), axis, 0, 0, tiled=True)
    return jnp.sum(parts, axis=0)


def sum_in_two_steps(shard, axes, dim):
    far, near = axes
    own = summed_on_arrival(split_up(shard, dim, lax.axis_size(far)), near, dim + 1)
    return jnp.sum(lax.all_to_all(own, far, 0, 0, tiled=True), axis=0)


def filled_up(lines, count):
    spare = -lines.shape[0] % count
    if not spare:
        return lines
    return jnp.concatenate([lines, jnp.zeros((spare, *lines.shape[1:]), lines.dtype)])


def sent_to_all(shard, axis):
    copies = jnp.broadcast_to(shard, (lax.axis_size(axis), *shard.shape))
    return lax.all_to_all(copies, axis, split_axis=0, concat_axis=0, tiled=True)


def in_order(parts, dim):
    shape = list(parts.shape[1:])
    shape[dim] *= parts.shape[0]
    return jnp.moveaxis(parts, 0, dim).reshape(shape)


def whole_of(shard, axes, dim):
    far, near = axes
    parts = sent_to_all(sent_to_all(shard, far), near)
    return in_order(parts.swapaxes(0, 1).reshape(-1, *shard.shape), dim)


def total_of(shard, axes):
    lines = shard.reshape(-1, shard.shape[-1])
    own = sum_in_two_steps(
        filled_up(lines, lax.axis_size(axes[0]) * lax.axis_size(axes[1])), axes, 0
    )
    whole = whole_of(own, axes, 0)
    return whole[: len(lines)].reshape(shard.shape)


def over_copies(shard, axis):
    everything = sent_to_all(shard, axis)
    return jnp.sum(everything, axis=0)


def local(outer_params, first_moment, second_moment, outer_moment, activations, targets):
    unit = lax.axis_index("grp")
    gathered = lax.all_gather(activations[0], "row", axis=1, tiled=True)
    wanted_all = targets[0]
    wanted_all = lax.all_gather(wanted_all, COL, axis=1, tiled=True)
    first = first_moment[0]
    second = second_moment[0]
    params = outer_params
    for inner_step in range(STEPS):
        inputs = gathered[inner_step]
        partial_value = jnp.dot(
            inputs, params.astype(jnp.bfloat16), preferred_element_type=jnp.float32
        )
        output = total_of(partial_value, (("col_0", "col_1"), "col_2"))
        residual = (output - wanted_all[inner_step].astype(jnp.float32)).astype(jnp.bfloat16)
        gradient = (
            lax.dot_general(
                inputs, residual, (((0,), (0,)), ((), ())), preferred_element_type=jnp.float32
            )
            / TOKENS
        )
        first_next = beta_first * first + (1.0 - beta_first) * gradient
        second_next = beta_second * second + (1.0 - beta_second) * gradient * gradient
        power = PRIOR + inner_step + 1
        corrected = (
            first_next
            / (1.0 - beta_first**power)
            / (jnp.sqrt(second_next / (1.0 - beta_second**power)) + epsilon_value)
        )
        params_next = params - inner_rate * (corrected + decay_rate * params)
        active = jnp.logical_or(unit < 3, inner_step < SLOW_STEPS)
        params = jnp.where(active, params_next, params)
        first = jnp.where(active, first_next, first)
        second = jnp.where(active, second_next, second)
    total_steps = float(3 * STEPS + SLOW_STEPS)
    weight = jnp.where(unit < 3, float(STEPS), float(SLOW_STEPS)) / total_steps
    term = weight * (outer_params - params)
    pseudo = over_copies(term, "grp")
    new_moment = momentum_coef * outer_moment + pseudo
    new_params = outer_params - outer_rate * (pseudo + momentum_coef * new_moment)
    return (new_params, new_moment)


def solution(mesh):
    finer = Mesh(
        mesh.devices.reshape(mesh.shape["grp"], mesh.shape["row"], 4, 2, 2),
        ("grp", "row", "col_0", "col_1", "col_2"),
    )
    placed = (
        P(COL, "row"),
        P("grp", COL, "row"),
        P("grp", COL, "row"),
        P(COL, "row"),
        P("grp", None, "row", COL),
        P("grp", None, COL, "row"),
    )
    return jax.shard_map(
        local,
        mesh=finer,
        in_specs=placed,
        out_specs=(P(COL, "row"), P(COL, "row")),
        check_vma=False,
    )
```

profile of v0, /device:TPU:1, one launch (start us, length us, event | category | flops | bytes accessed | tf_op | source)
XLA Modules:
  0.0 409.2 jit_solution(15068283860982565642)
XLA Ops:
  7.2 0.7 all-gather.5.cloned.1.call-update
  7.9 0.7 all-gather.7.cloned.1.call-update
  8.7 73.2 %all-gather.5.cloned.1.call-done = bf16[1,3,2048,512]{3,2,1,0:T(8,128)(2,1)} async-done(((bf16[1,3,512,512]{3,2,1,0:T(8,128)(2,1)}), bf16[1,3,2048,512]{3,2,1,0:T(8,128)(2,1)}) %all-gather.5.cloned.1.call-update) | async-done | bytes 6291472 | tf_op jit(solution)/shard_map/all_gather | solution.py:78
  81.8 1.6 slice-done.6
  83.4 0.7 convolution_bitcast_fusion.2
  84.1 0.2 copy.76
  84.3 5.8 %all_to_all.65 = f32[2,8,128,256]{3,2,1,0:T(8,128)S(1)} all-to-all(f32[2,8,128,256]{3,2,1,0:T(8,128)S(1)} %copy.76), channel_id=1, replica_groups=mesh['grp'=4,'row'=4,'col_0'=4,'col_1'=2,'col_2'=2] {'col_2'}, dimensions={0} | all-to-all | bytes 4194304 | tf_op jit(solution)/shard_map/all_to_all | solution.py:28
  90.1 0.2 reduce_sum.63
  90.3 35.3 %all_to_all.66 = f32[8,128,256]{2,1,0:T(8,128)S(1)} all-to-all(f32[8,128,256]{2,1,0:T(8,128)S(1)} %reduce_sum.63), channel_id=1, replica_groups=mesh['grp'=4,'row'=4,'col_0'=4,'col_1'=2,'col_2'=2] {'col_0','col_1'}, dimensions={0} | all-to-all | bytes 2097152 | tf_op jit(solution)/shard_map/all_to_all | solution.py:35
  125.7 1.1 broadcast_in_dim.21
  126.8 7.7 %all-to-all-start.2 = ((f32[8,128,256]{2,1,0:T(8,128)}), f32[8,128,256]{2,1,0:T(8,128)S(1)}, u32[]{:S(2)}, u32[]{:S(2)}) async-start(f32[8,128,256]{2,1,0:T(8,128)} %broadcast_in_dim.21), calls=%async_computation.2 | async-start | bytes 2097152 | tf_op jit(solution)/shard_map/all_to_all | solution.py:47
  134.6 0.2 copy.98
  134.8 1.0 copy.75
  135.8 0.2 copy.78
  136.0 35.4 %all-gather.7.cloned.1.call-done = bf16[1,3,2048,256]{3,2,1,0:T(8,128)(2,1)} async-done(((bf16[1,3,128,256]{3,2,1,0:T(8,128)(2,1)}), bf16[1,3,2048,256]{3,2,1,0:T(8,128)(2,1)}) %all-gather.7.cloned.1.call-update) | async-done | bytes 3145744 | tf_op jit(solution)/shard_map/all_gather | solution.py:80
  171.4 3.4 fusion.43
  174.8 0.2 broadcast_in_dim.22
  175.0 5.7 %all_to_all.67 = f32[2,8,128,256]{3,2,1,0:T(8,128)S(1)} all-to-all(f32[2,8,128,256]{3,2,1,0:T(8,128)S(1)} %broadcast_in_dim.22), channel_id=1, replica_groups=mesh['grp'=4,'row'=4,'col_0'=4,'col_1'=2,'col_2'=2] {'col_2'}, dimensions={0} | all-to-all | bytes 4194304 | tf_op jit(solution)/shard_map/all_to_all | solution.py:47
  180.7 0.4 fusion.2
  181.1 0.7 fusion.3
  181.9 0.9 copy-done.15
  182.7 2.4 convolution_bitcast_fusion.1
  185.2 3.0 reshape_reshape.4
  188.2 0.1 copy.112
  188.3 5.4 %all_to_all.68 = f32[2,8,128,256]{2,1,3,0:T(8,128)S(1)} all-to-all(f32[2,8,128,256]{2,1,3,0:T(8,128)S(1)} %bitcast.148), channel_id=1, replica_groups=mesh['grp'=4,'row'=4,'col_0'=4,'col_1'=2,'col_2'=2] {'col_2'}, dimensions={0} | all-to-all | bytes 4194304 | tf_op jit(solution)/shard_map/all_to_all | solution.py:28
  193.8 0.2 reduce_sum.65
  194.0 0.2 copy.83
  194.2 21.3 %all_to_all.69 = f32[8,128,256]{1,2,0:T(8,128)S(1)} all-to-all(f32[8,128,256]{1,2,0:T(8,128)S(1)} %copy.83), channel_id=1, replica_groups=mesh['grp'=4,'row'=4,'col_0'=4,'col_1'=2,'col_2'=2] {'col_0','col_1'}, dimensions={0} | all-to-all | bytes 2097152 | tf_op jit(solution)/shard_map/all_to_all | solution.py:35
  215.7 1.0 broadcast_in_dim.23
  216.7 3.6 all-to-all-start.6
  220.3 24.7 %all-to-all-done.6 = f32[8,128,256]{2,1,0:T(8,128)S(1)} async-done(((f32[8,128,256]{2,1,0:T(8,128)}), f32[8,128,256]{2,1,0:T(8,128)S(1)}, u32[]{:S(2)}, u32[]{:S(2)}) %all-to-all-start.6) | async-done | bytes 1048608 | tf_op jit(solution)/shard_map/all_to_all | solution.py:47
  245.0 0.2 broadcast_in_dim.24
  245.2 6.0 %all_to_all.70 = f32[2,8,128,256]{3,2,1,0:T(8,128)S(1)} all-to-all(f32[2,8,128,256]{3,2,1,0:T(8,128)S(1)} %broadcast_in_dim.24), channel_id=1, replica_groups=mesh['grp'=4,'row'=4,'col_0'=4,'col_1'=2,'col_2'=2] {'col_2'}, dimensions={0} | all-to-all | bytes 4194304 | tf_op jit(solution)/shard_map/all_to_all | solution.py:47
  251.2 0.3 fusion.1
  251.6 0.7 fusion.5
  252.3 0.8 copy-done.18
  253.1 2.9 convolution_bitcast_fusion
  256.0 3.0 reshape_reshape.5
  259.2 5.4 %all_to_all.71 = f32[2,8,128,256]{2,1,3,0:T(8,128)S(1)} all-to-all(f32[2,8,128,256]{2,1,3,0:T(8,128)S(1)} %bitcast.149), channel_id=1, replica_groups=mesh['grp'=4,'row'=4,'col_0'=4,'col_1'=2,'col_2'=2] {'col_2'}, dimensions={0} | all-to-all | bytes 4194304 | tf_op jit(solution)/shard_map/all_to_all | solution.py:28
  264.6 0.2 reduce_sum.67
  264.9 0.2 copy.89
  265.1 25.3 %all_to_all.72 = f32[8,128,256]{1,2,0:T(8,128)S(1)} all-to-all(f32[8,128,256]{1,2,0:T(8,128)S(1)} %copy.89), channel_id=1, replica_groups=mesh['grp'=4,'row'=4,'col_0'=4,'col_1'=2,'col_2'=2] {'col_0','col_1'}, dimensions={0} | all-to-all | bytes 2097152 | tf_op jit(solution)/shard_map/all_to_all | solution.py:35
  290.5 1.0 broadcast_in_dim.25
  291.5 3.6 all-to-all-start.10
  295.1 20.5 %all-to-all-done.10 = f32[8,128,256]{2,1,0:T(8,128)S(1)} async-done(((f32[8,128,256]{2,1,0:T(8,128)}), f32[8,128,256]{2,1,0:T(8,128)S(1)}, u32[]{:S(2)}, u32[]{:S(2)}) %all-to-all-start.10) | async-done | bytes 1048608 | tf_op jit(solution)/shard_map/all_to_all | solution.py:47
  315.6 0.2 broadcast_in_dim.26
  315.8 6.9 %all_to_all.73 = f32[2,8,128,256]{3,2,1,0:T(8,128)S(1)} all-to-all(f32[2,8,128,256]{3,2,1,0:T(8,128)S(1)} %broadcast_in_dim.26), channel_id=1, replica_groups=mesh['grp'=4,'row'=4,'col_0'=4,'col_1'=2,'col_2'=2] {'col_2'}, dimensions={0} | all-to-all | bytes 4194304 | tf_op jit(solution)/shard_map/all_to_all | solution.py:47
  322.8 0.3 fusion
  323.1 0.7 copy-done.6
  323.8 0.2 copy-done.11
  323.9 0.2 copy-done.14
  324.1 0.2 copy-done.17
  324.3 0.2 copy-done.19
  324.4 3.4 fusion.8
  327.8 0.2 copy.94
  328.0 1.5 broadcast_in_dim.27
  329.5 20.7 %all-to-all-start.12 = ((f32[4,512,256]{2,1,0:T(8,128)}), f32[4,512,256]{2,1,0:T(8,128)S(1)}, u32[]{:S(2)}, u32[]{:S(2)}) async-start(f32[4,512,256]{2,1,0:T(8,128)} %broadcast_in_dim.27), calls=%async_computation.12 | async-start | bytes 4194304 | tf_op jit(solution)/shard_map/all_to_all | solution.py:47
  350.3 1.2 copy.95
  351.5 46.5 %all-to-all-done.12 = f32[4,512,256]{2,1,0:T(8,128)S(1)} async-done(((f32[4,512,256]{2,1,0:T(8,128)}), f32[4,512,256]{2,1,0:T(8,128)S(1)}, u32[]{:S(2)}, u32[]{:S(2)}) %all-to-all-start.12) | async-done | bytes 2097184 | tf_op jit(solution)/shard_map/all_to_all | solution.py:47
  398.0 1.0 reduce_sum.69
  399.0 1.2 copy.97
  400.2 0.2 multiply_add_fusion
  400.4 1.0 copy.99
  401.4 1.0 copy.100
  (58 shorter events, 0.7 us)
Async XLA Ops:
  7.2 74.7 %all-gather.5.cloned.1.call-start = ((), (), s32[]{:S(2)}) async-start(), calls=%async_computation.13 | async-start | bytes 7864320 | tf_op jit(solution)/shard_map/all_gather | solution.py:78
  7.9 163.5 %all-gather.7.cloned.1.call-start = ((), (), s32[]{:S(2)}) async-start(), calls=%async_computation.14 | async-start | bytes 3342336 | tf_op jit(solution)/shard_map/all_gather | solution.py:80
  8.6 73.2 %copy-start.2 = (f32[512,256]{1,0:T(8,128)S(1)}, f32[512,256]{1,0:T(8,128)}, u32[]{:S(2)}) copy-start(f32[512,256]{1,0:T(8,128)} %param.6) | copy-start | bytes 1572868
  81.8 1.6 slice-start.6
  125.6 8.9 %copy-start.3 = (f32[512,256]{1,0:T(8,128)S(1)}, f32[512,256]{1,0:T(8,128)}, u32[]{:S(2)}) copy-start(f32[512,256]{1,0:T(8,128)} %param.6) | copy-start | bytes 1572868
  125.7 9.1 %copy-start.7 = (f32[1,512,256]{2,1,0:T(8,128)S(1)}, f32[1,512,256]{2,1,0:T(8,128)}, u32[]{:S(2)}) copy-start(f32[1,512,256]{2,1,0:T(8,128)} %param.7) | copy-start | bytes 1572868
  126.8 9.0 %copy-start.8 = (f32[1,512,256]{2,1,0:T(8,128)S(1)}, f32[1,512,256]{2,1,0:T(8,128)}, u32[]{:S(2)}) copy-start(f32[1,512,256]{2,1,0:T(8,128)} %param.8) | copy-start | bytes 1572868
  126.8 47.9 %all-to-all-start.2 = ((f32[8,128,256]{2,1,0:T(8,128)}), f32[8,128,256]{2,1,0:T(8,128)S(1)}, u32[]{:S(2)}, u32[]{:S(2)}) async-start(f32[8,128,256]{2,1,0:T(8,128)} %broadcast_in_dim.21), calls=%async_computation.2 | async-start | bytes 2097152 | tf_op jit(solution)/shard_map/all_to_all | solution.py:47
  134.8 47.1 %copy-start.4 = (f32[512,256]{0,1:T(8,128)}, f32[512,256]{0,1:T(8,128)S(1)}, u32[]{:S(2)}) copy-start(f32[512,256]{0,1:T(8,128)S(1)} %copy.98) | copy-start | bytes 1572868
  136.0 45.9 %copy-start.12 = (f32[1,512,256]{1,2,0:T(8,128)}, f32[1,512,256]{1,2,0:T(8,128)S(1)}, u32[]{:S(2)}) copy-start(f32[1,512,256]{1,2,0:T(8,128)S(1)} %copy.78) | copy-start | bytes 1572868
  174.8 6.3 %slice-start = ((s8[6291456]{0:T(1024)(128)(4,1)}), s8[4194304]{0:T(1024)(128)(4,1)S(1)}, s32[]{:S(2)}) async-start(s8[6291456]{0:T(1024)(128)(4,1)} %bitcast.150), calls=%async_computation.15 | async-start | bytes 8388608
  175.0 6.1 %slice-start.1 = ((s8[6291456]{0:T(1024)(128)(4,1)}), s8[2097152]{0:T(1024)(128)(4,1)S(1)}, s32[]{:S(2)}) async-start(s8[6291456]{0:T(1024)(128)(4,1)} %bitcast.150), calls=%async_computation.16 | async-start | bytes 4194304
  181.1 1.6 copy-start.9
  181.9 0.9 copy-start.15
  216.7 28.3 %all-to-all-start.6 = ((f32[8,128,256]{2,1,0:T(8,128)}), f32[8,128,256]{2,1,0:T(8,128)S(1)}, u32[]{:S(2)}, u32[]{:S(2)}) async-start(f32[8,128,256]{2,1,0:T(8,128)} %broadcast_in_dim.23), calls=%async_computation.6 | async-start | bytes 2097152 | tf_op jit(solution)/shard_map/all_to_all | solution.py:47
  245.0 6.5 %slice-start.2 = ((s8[6291456]{0:T(1024)(128)(4,1)}), s8[4194304]{0:T(1024)(128)(4,1)S(1)}, s32[]{:S(2)}) async-start(s8[6291456]{0:T(1024)(128)(4,1)} %bitcast.152), calls=%async_computation.17 | async-start | bytes 8388608
  245.2 6.0 %copy-start.1 = (bf16[1,1,2048,256]{3,2,1,0:T(8,128)(2,1)S(1)}, bf16[1,1,2048,256]{3,2,1,0:T(8,128)(2,1)}, u32[]{:S(2)}) copy-start(bf16[1,1,2048,256]{3,2,1,0:T(8,128)(2,1)} %get-tuple-element.13) | copy-start | bytes 3145732
  245.2 6.3 %slice-start.3 = ((s8[6291456]{0:T(1024)(128)(4,1)}), s8[2097152]{0:T(1024)(128)(4,1)S(1)}, s32[]{:S(2)}) async-start(s8[6291456]{0:T(1024)(128)(4,1)} %bitcast.152), calls=%async_computation.18 | async-start | bytes 4194304
  251.6 1.6 copy-start.5
  251.6 1.6 copy-start.10
  251.6 1.5 copy-start.13
  251.6 1.5 copy-start.16
  252.3 0.8 copy-start.18
  291.5 24.0 %all-to-all-start.10 = ((f32[8,128,256]{2,1,0:T(8,128)}), f32[8,128,256]{2,1,0:T(8,128)S(1)}, u32[]{:S(2)}, u32[]{:S(2)}) async-start(f32[8,128,256]{2,1,0:T(8,128)} %broadcast_in_dim.25), calls=%async_computation.10 | async-start | bytes 2097152 | tf_op jit(solution)/shard_map/all_to_all | solution.py:47
  315.6 7.5 %slice-start.4 = ((s8[6291456]{0:T(1024)(128)(4,1)}), s8[4194304]{0:T(1024)(128)(4,1)S(1)}, s32[]{:S(2)}) async-start(s8[6291456]{0:T(1024)(128)(4,1)} %bitcast.154), calls=%async_computation.19 | async-start | bytes 8388608
  315.8 6.9 %copy-start = (bf16[1,1,2048,256]{3,2,1,0:T(8,128)(2,1)S(1)}, bf16[1,1,2048,256]{3,2,1,0:T(8,128)(2,1)}, u32[]{:S(2)}) copy-start(bf16[1,1,2048,256]{3,2,1,0:T(8,128)(2,1)} %get-tuple-element.14) | copy-start | bytes 3145732
  315.8 7.3 %slice-start.5 = ((s8[6291456]{0:T(1024)(128)(4,1)}), s8[2097152]{0:T(1024)(128)(4,1)S(1)}, s32[]{:S(2)}) async-start(s8[6291456]{0:T(1024)(128)(4,1)} %bitcast.154), calls=%async_computation.20 | async-start | bytes 4194304
  322.7 1.0 copy-start.6
  322.7 1.2 copy-start.11
  322.7 1.4 copy-start.14
  322.7 1.5 copy-start.17
  322.8 1.7 copy-start.19
  329.5 68.5 %all-to-all-start.12 = ((f32[4,512,256]{2,1,0:T(8,128)}), f32[4,512,256]{2,1,0:T(8,128)S(1)}, u32[]{:S(2)}, u32[]{:S(2)}) async-start(f32[4,512,256]{2,1,0:T(8,128)} %broadcast_in_dim.27), calls=%async_computation.12 | async-start | bytes 4194304 | tf_op jit(solution)/shard_map/all_to_all | solution.py:47
Sparse Core Ops, SparseCore 0:
  9.8 71.9 all-gather.4
  84.6 86.7 all-gather.6
where the time goes:
time: 410 us; the launch traced here: 409 us
  waiting for transfers between devices  202 us (49%)
  blocking collectives  117 us (29%)
  starting transfers between devices  35.7 us (9%)
  local copies, waits for them, and re-layouts  26.5 us (6%)
  between operations  14.6 us (4%)
  matrix products  10.9 us (3%)
    all_to_all x4, waiting for transfers between devices, sent_to_all(): return lax.all_to_all(copies, axis, split_axis=0, concat_axis=0, tiled=True)  91.7 us
    all_to_all x3, blocking collectives, sum_in_two_steps(): return jnp.sum(lax.all_to_all(own, far, 0, 0, tiled=True), axis=0)  81.9 us
    all_gather x1, waiting for transfers between devices, local(): gathered = lax.all_gather(activations[0], 'row', axis=1, tiled=True)  73.2 us
    all_to_all x4, starting transfers between devices, sent_to_all(): return lax.all_to_all(copies, axis, split_axis=0, concat_axis=0, tiled=True)  35.6 us
    all_gather x1, waiting for transfers between devices, local(): wanted_all = lax.all_gather(wanted_all, COL, axis=1, tiled=True)  35.4 us
    all_to_all x3, blocking collectives, sent_to_all(): return lax.all_to_all(copies, axis, split_axis=0, concat_axis=0, tiled=True)  18.6 us
    all_to_all x3, blocking collectives, summed_on_arrival(): parts = lax.all_to_all(split_up(shard, dim, count), axis, 0, 0, tiled=True)  16.6 us
  transfers between devices with their start and end apart: 6, of which 5 were waited for; matrix products, arithmetic and copies ran while one was open for 2% of the time, Pallas kernels for 0%

commit v1 on v0

--- a/solution.py
+++ b/solution.py
@@ -77,7 +77,9 @@
     unit = lax.axis_index("grp")
     gathered = lax.all_gather(activations[0], "row", axis=1, tiled=True)
     wanted_all = targets[0]
-    wanted_all = lax.all_gather(wanted_all, COL, axis=1, tiled=True)
+    wanted_all = jnp.concatenate(
+        lax.all_to_all(jnp.stack([wanted_all] * lax.axis_size(COL), axis=0), COL, 0, 0), axis=1
+    )
     first = first_moment[0]
     second = second_moment[0]
     params = outer_params

time: 410 us -> 483 us (1.18)
  starting transfers between devices: 35.7 us -> 74.2 us
  blocking collectives: 117 us -> 145 us
  local copies, waits for them, and re-layouts: 26.5 us -> 33.2 us
    all_to_all x0 -> x1, waiting for transfers between devices: none -> 41.5 us  [local(): lax.all_to_all(jnp.stack([wanted_all] * lax.axis_size(COL), axis=0), COL,...]
    all_gather x1 -> x0, waiting for transfers between devices: 35.4 us -> none  [local(): wanted_all = lax.all_gather(wanted_all, COL, axis=1, tiled=True)]
    all_to_all x4, starting transfers between devices: 35.6 us -> 67.8 us  [sent_to_all(): return lax.all_to_all(copies, axis, split_axis=0, concat_axis=0, tiled=True)]
    all_to_all x3, blocking collectives: 18.6 us -> 40.9 us  [sent_to_all(): return lax.all_to_all(copies, axis, split_axis=0, concat_axis=0, tiled=True)]
    all_to_all x4, waiting for transfers between devices: 91.7 us -> 83.8 us  [sent_to_all(): return lax.all_to_all(copies, axis, split_axis=0, concat_axis=0, tiled=True)]
    all_to_all x0 -> x1, starting transfers between devices: none -> 6.3 us  [local(): lax.all_to_all(jnp.stack([wanted_all] * lax.axis_size(COL), axis=0), COL,...]
    all_to_all x3, blocking collectives: 81.9 us -> 87.2 us  [sum_in_two_steps(): return jnp.sum(lax.all_to_all(own, far, 0, 0, tiled=True), axis=0)]
    unnamed x58 -> x54, local copies, waits for them, and re-layouts: 7.66 us -> 12.3 us
  transfers between devices with their start and end apart: 6 -> 6, of which waited for: 5 -> 6; matrix products, arithmetic and copies ran while one was open for 2% -> 2% of each run, Pallas kernels for 0% -> 0%
where the time goes in v1:
time: 483 us; the launch traced here: 482 us
  waiting for transfers between devices  200 us (41%)
  blocking collectives  145 us (30%)
  starting transfers between devices  74.2 us (15%)
  local copies, waits for them, and re-layouts  33.2 us (7%)
  between operations  14.5 us (3%)
  matrix products  10.9 us (2%)
    all_to_all x3, blocking collectives, sum_in_two_steps(): return jnp.sum(lax.all_to_all(own, far, 0, 0, tiled=True), axis=0)  87.2 us
    all_to_all x4, waiting for transfers between devices, sent_to_all(): return lax.all_to_all(copies, axis, split_axis=0, concat_axis=0, tiled=True)  83.8 us
    all_gather x1, waiting for transfers between devices, local(): gathered = lax.all_gather(activations[0], 'row', axis=1, tiled=True)  73.9 us
    all_to_all x4, starting transfers between devices, sent_to_all(): return lax.all_to_all(copies, axis, split_axis=0, concat_axis=0, tiled=True)  67.8 us
    all_to_all x1, waiting for transfers between devices, local(): lax.all_to_all(jnp.stack([wanted_all] * lax.axis_size(COL), axis=0), COL,...  41.5 us
    all_to_all x3, blocking collectives, sent_to_all(): return lax.all_to_all(copies, axis, split_axis=0, concat_axis=0, tiled=True)  40.9 us
    all_to_all x3, blocking collectives, summed_on_arrival(): parts = lax.all_to_all(split_up(shard, dim, count), axis, 0, 0, tiled=True)  16.6 us
    unnamed x54, local copies, waits for them, and re-layouts  12.3 us
  transfers between devices with their start and end apart: 6, of which 6 were waited for; matrix products, arithmetic and copies ran while one was open for 2% of the time, Pallas kernels for 0%

profile of v1, /device:TPU:1, one launch (start us, length us, event | category | flops | bytes accessed | tf_op | source)
XLA Modules:
  0.0 481.5 jit_solution(14510557006877656897)
XLA Ops:
  7.2 0.7 all-gather.3.cloned.1.call-update
  7.9 73.9 %all-gather.3.cloned.1.call-done = bf16[1,3,2048,512]{3,2,1,0:T(8,128)(2,1)} async-done(((bf16[1,3,512,512]{3,2,1,0:T(8,128)(2,1)}), bf16[1,3,2048,512]{3,2,1,0:T(8,128)(2,1)}) %all-gather.3.cloned.1.call-update) | async-done | bytes 6291472 | tf_op jit(solution)/shard_map/all_gather | solution.py:78
  81.8 1.6 slice-done.6
  83.4 0.7 convolution_bitcast_fusion.2
  84.1 0.2 copy.92
  84.3 5.8 %all_to_all.70 = f32[2,8,128,256]{3,2,1,0:T(8,128)S(1)} all-to-all(f32[2,8,128,256]{3,2,1,0:T(8,128)S(1)} %copy.92), channel_id=1, replica_groups=mesh['grp'=4,'row'=4,'col_0'=4,'col_1'=2,'col_2'=2] {'col_2'}, dimensions={0} | all-to-all | bytes 4194304 | tf_op jit(solution)/shard_map/all_to_all | solution.py:28
  90.1 0.2 reduce_sum.63
  90.3 33.6 %all_to_all.71 = f32[8,128,256]{2,1,0:T(8,128)} all-to-all(f32[8,128,256]{2,1,0:T(8,128)S(1)} %reduce_sum.63), channel_id=1, replica_groups=mesh['grp'=4,'row'=4,'col_0'=4,'col_1'=2,'col_2'=2] {'col_0','col_1'}, dimensions={0} | all-to-all | bytes 2097152 | tf_op jit(solution)/shard_map/all_to_all | solution.py:35
  123.9 2.1 stack.3
  126.0 6.3 %all-to-all-start.4 = ((bf16[16,3,128,256]{3,2,1,0:T(8,128)(2,1)}), bf16[16,3,128,256]{3,2,1,0:T(8,128)(2,1)S(1)}, u32[]{:S(2)}, u32[]{:S(2)}) async-start(bf16[16,3,128,256]{3,2,1,0:T(8,128)(2,1)} %stack.3), calls=%async_computation.4 | async-start | bytes 6291456 | tf_op jit(solution)/shard_map/all_to_all | solution.py:81
  132.3 1.3 reduce_sum.64
  133.6 41.5 %all-to-all-done.4 = bf16[16,3,128,256]{3,2,1,0:T(8,128)(2,1)S(1)} async-done(((bf16[16,3,128,256]{3,2,1,0:T(8,128)(2,1)}), bf16[16,3,128,256]{3,2,1,0:T(8,128)(2,1)S(1)}, u32[]{:S(2)}, u32[]{:S(2)}) %all-to-all-start.4) | async-done | bytes 3145760 | tf_op jit(solution)/shard_map/all_to_all | solution.py:81
  175.1 1.2 broadcast_in_dim.21
  176.3 35.7 %all-to-all-start.2 = ((f32[8,128,256]{2,1,0:T(8,128)}), f32[8,128,256]{2,1,0:T(8,128)}, u32[]{:S(2)}, u32[]{:S(2)}) async-start(f32[8,128,256]{2,1,0:T(8,128)} %broadcast_in_dim.21), calls=%async_computation.2 | async-start | bytes 2097152 | tf_op jit(solution)/shard_map/all_to_all | solution.py:47
  212.0 2.0 copy.115
  214.0 2.0 copy.91
  216.0 2.1 copy.95
  218.1 0.2 copy.129
  218.3 1.7 fusion.43
  220.0 8.8 %all-to-all-done.2 = f32[8,128,256]{2,1,0:T(8,128)} async-done(((f32[8,128,256]{2,1,0:T(8,128)}), f32[8,128,256]{2,1,0:T(8,128)}, u32[]{:S(2)}, u32[]{:S(2)}) %all-to-all-start.2) | async-done | bytes 1048608 | tf_op jit(solution)/shard_map/all_to_all | solution.py:47
  228.8 1.6 broadcast_in_dim.22
  230.4 9.1 %all_to_all.72 = f32[2,8,128,256]{3,2,1,0:T(8,128)S(1)} all-to-all(f32[2,8,128,256]{3,2,1,0:T(8,128)S(1)} %broadcast_in_dim.22), channel_id=1, replica_groups=mesh['grp'=4,'row'=4,'col_0'=4,'col_1'=2,'col_2'=2] {'col_2'}, dimensions={0} | all-to-all | bytes 4194304 | tf_op jit(solution)/shard_map/all_to_all | solution.py:47
  239.5 0.4 fusion.2
  240.0 0.7 fusion.3
  240.7 0.8 copy-done.13
  241.5 2.4 convolution_bitcast_fusion.1
  243.9 3.0 reshape_reshape.4
  247.1 5.4 %all_to_all.73 = f32[2,8,128,256]{2,1,3,0:T(8,128)S(1)} all-to-all(f32[2,8,128,256]{2,1,3,0:T(8,128)S(1)} %bitcast.153), channel_id=1, replica_groups=mesh['grp'=4,'row'=4,'col_0'=4,'col_1'=2,'col_2'=2] {'col_2'}, dimensions={0} | all-to-all | bytes 4194304 | tf_op jit(solution)/shard_map/all_to_all | solution.py:28
  252.5 0.2 reduce_sum.65
  252.8 0.2 copy.100
  253.0 30.9 %all_to_all.74 = f32[8,128,256]{1,2,0:T(8,128)S(1)} all-to-all(f32[8,128,256]{1,2,0:T(8,128)S(1)} %copy.100), channel_id=1, replica_groups=mesh['grp'=4,'row'=4,'col_0'=4,'col_1'=2,'col_2'=2] {'col_0','col_1'}, dimensions={0} | all-to-all | bytes 2097152 | tf_op jit(solution)/shard_map/all_to_all | solution.py:35
  284.0 1.0 broadcast_in_dim.23
  285.1 3.6 all-to-all-start.7
  288.6 14.2 %all-to-all-done.7 = f32[8,128,256]{2,1,0:T(8,128)S(1)} async-done(((f32[8,128,256]{2,1,0:T(8,128)}), f32[8,128,256]{2,1,0:T(8,128)S(1)}, u32[]{:S(2)}, u32[]{:S(2)}) %all-to-all-start.7) | async-done | bytes 1048608 | tf_op jit(solution)/shard_map/all_to_all | solution.py:47
  302.8 0.2 broadcast_in_dim.24
  303.1 16.8 %all_to_all.75 = f32[2,8,128,256]{3,2,1,0:T(8,128)S(1)} all-to-all(f32[2,8,128,256]{3,2,1,0:T(8,128)S(1)} %broadcast_in_dim.24), channel_id=1, replica_groups=mesh['grp'=4,'row'=4,'col_0'=4,'col_1'=2,'col_2'=2] {'col_2'}, dimensions={0} | all-to-all | bytes 4194304 | tf_op jit(solution)/shard_map/all_to_all | solution.py:47
  319.8 0.3 fusion.1
  320.2 0.7 fusion.5
  321.0 0.8 copy-done.16
  321.8 2.9 convolution_bitcast_fusion
  324.7 3.0 reshape_reshape.5
  327.8 5.4 %all_to_all.76 = f32[2,8,128,256]{2,1,3,0:T(8,128)S(1)} all-to-all(f32[2,8,128,256]{2,1,3,0:T(8,128)S(1)} %bitcast.154), channel_id=1, replica_groups=mesh['grp'=4,'row'=4,'col_0'=4,'col_1'=2,'col_2'=2] {'col_2'}, dimensions={0} | all-to-all | bytes 4194304 | tf_op jit(solution)/shard_map/all_to_all | solution.py:28
  333.3 0.2 reduce_sum.67
  333.5 0.2 copy.106
  333.7 22.7 %all_to_all.77 = f32[8,128,256]{1,2,0:T(8,128)S(1)} all-to-all(f32[8,128,256]{1,2,0:T(8,128)S(1)} %copy.106), channel_id=1, replica_groups=mesh['grp'=4,'row'=4,'col_0'=4,'col_1'=2,'col_2'=2] {'col_0','col_1'}, dimensions={0} | all-to-all | bytes 2097152 | tf_op jit(solution)/shard_map/all_to_all | solution.py:35
  356.6 1.0 broadcast_in_dim.25
  357.6 3.7 all-to-all-start.11
  361.4 14.3 %all-to-all-done.11 = f32[8,128,256]{2,1,0:T(8,128)S(1)} async-done(((f32[8,128,256]{2,1,0:T(8,128)}), f32[8,128,256]{2,1,0:T(8,128)S(1)}, u32[]{:S(2)}, u32[]{:S(2)}) %all-to-all-start.11) | async-done | bytes 1048608 | tf_op jit(solution)/shard_map/all_to_all | solution.py:47
  375.7 0.2 broadcast_in_dim.26
  375.9 15.0 %all_to_all.78 = f32[2,8,128,256]{3,2,1,0:T(8,128)S(1)} all-to-all(f32[2,8,128,256]{3,2,1,0:T(8,128)S(1)} %broadcast_in_dim.26), channel_id=1, replica_groups=mesh['grp'=4,'row'=4,'col_0'=4,'col_1'=2,'col_2'=2] {'col_2'}, dimensions={0} | all-to-all | bytes 4194304 | tf_op jit(solution)/shard_map/all_to_all | solution.py:47
  391.0 0.3 fusion
  391.3 0.7 copy-done.5
  392.5 0.2 copy-done.17
  392.6 3.4 fusion.8
  396.1 0.2 copy.111
  396.3 1.5 broadcast_in_dim.27
  397.8 24.8 %all-to-all-start.13 = ((f32[4,512,256]{2,1,0:T(8,128)}), f32[4,512,256]{2,1,0:T(8,128)S(1)}, u32[]{:S(2)}, u32[]{:S(2)}) async-start(f32[4,512,256]{2,1,0:T(8,128)} %broadcast_in_dim.27), calls=%async_computation.13 | async-start | bytes 4194304 | tf_op jit(solution)/shard_map/all_to_all | solution.py:47
  422.6 1.2 copy.112
  423.8 46.5 %all-to-all-done.13 = f32[4,512,256]{2,1,0:T(8,128)S(1)} async-done(((f32[4,512,256]{2,1,0:T(8,128)}), f32[4,512,256]{2,1,0:T(8,128)S(1)}, u32[]{:S(2)}, u32[]{:S(2)}) %all-to-all-start.13) | async-done | bytes 2097184 | tf_op jit(solution)/shard_map/all_to_all | solution.py:47
  470.3 1.0 reduce_sum.69
  471.3 1.2 copy.114
  472.5 0.2 multiply_add_fusion
  472.7 1.0 copy.116
  473.7 1.0 copy.117
  (55 shorter events, 1.2 us)
Async XLA Ops:
  7.2 74.7 %all-gather.3.cloned.1.call-start = ((), (), s32[]{:S(2)}) async-start(), calls=%async_computation.14 | async-start | bytes 7864320 | tf_op jit(solution)/shard_map/all_gather | solution.py:78
  7.9 73.9 %copy-start.2 = (f32[512,256]{1,0:T(8,128)S(1)}, f32[512,256]{1,0:T(8,128)}, u32[]{:S(2)}) copy-start(f32[512,256]{1,0:T(8,128)} %param.6) | copy-start | bytes 1572868
  81.8 1.6 slice-start.6
  90.1 33.8 %copy-start.12 = (bf16[1,3,128,256]{3,2,1,0:T(8,128)(2,1)S(1)}, bf16[1,3,128,256]{3,2,1,0:T(8,128)(2,1)}, u32[]{:S(2)}) copy-start(bf16[1,3,128,256]{3,2,1,0:T(8,128)(2,1)} %param.11) | copy-start | bytes 589828
  126.0 49.1 %all-to-all-start.4 = ((bf16[16,3,128,256]{3,2,1,0:T(8,128)(2,1)}), bf16[16,3,128,256]{3,2,1,0:T(8,128)(2,1)S(1)}, u32[]{:S(2)}, u32[]{:S(2)}) async-start(bf16[16,3,128,256]{3,2,1,0:T(8,128)(2,1)} %stack.3), calls=%async_computation.4 | async-start | bytes 6291456 | tf_op jit(solution)/shard_map/all_to_all | solution.py:81
  176.3 52.6 %all-to-all-start.2 = ((f32[8,128,256]{2,1,0:T(8,128)}), f32[8,128,256]{2,1,0:T(8,128)}, u32[]{:S(2)}, u32[]{:S(2)}) async-start(f32[8,128,256]{2,1,0:T(8,128)} %broadcast_in_dim.21), calls=%async_computation.2 | async-start | bytes 2097152 | tf_op jit(solution)/shard_map/all_to_all | solution.py:47
  228.8 11.1 %slice-start = ((s8[6291456]{0:T(1024)(128)(4,1)}), s8[4194304]{0:T(1024)(128)(4,1)S(1)}, s32[]{:S(2)}) async-start(s8[6291456]{0:T(1024)(128)(4,1)} %bitcast.155), calls=%async_computation.15 | async-start | bytes 8388608
  230.4 9.5 %slice-start.1 = ((s8[6291456]{0:T(1024)(128)(4,1)}), s8[2097152]{0:T(1024)(128)(4,1)S(1)}, s32[]{:S(2)}) async-start(s8[6291456]{0:T(1024)(128)(4,1)} %bitcast.155), calls=%async_computation.16 | async-start | bytes 4194304
  239.9 1.6 copy-start.3
  240.0 1.6 copy-start.6
  240.0 1.5 copy-start.9
  240.7 0.8 copy-start.13
  285.1 17.8 %all-to-all-start.7 = ((f32[8,128,256]{2,1,0:T(8,128)}), f32[8,128,256]{2,1,0:T(8,128)S(1)}, u32[]{:S(2)}, u32[]{:S(2)}) async-start(f32[8,128,256]{2,1,0:T(8,128)} %broadcast_in_dim.23), calls=%async_computation.7 | async-start | bytes 2097152 | tf_op jit(solution)/shard_map/all_to_all | solution.py:47
  302.8 17.4 %slice-start.2 = ((s8[6291456]{0:T(1024)(128)(4,1)}), s8[4194304]{0:T(1024)(128)(4,1)S(1)}, s32[]{:S(2)}) async-start(s8[6291456]{0:T(1024)(128)(4,1)} %bitcast.157), calls=%async_computation.17 | async-start | bytes 8388608
  303.0 16.8 %copy-start.1 = (bf16[1,16,128,256]{3,2,1,0:T(8,128)(2,1)S(1)}, bf16[1,16,128,256]{3,2,1,0:T(8,128)(2,1)}, u32[]{:S(2)}) copy-start(bf16[1,16,128,256]{3,2,1,0:T(8,128)(2,1)} %get-tuple-element.16) | copy-start | bytes 3145732
  303.0 17.1 %slice-start.3 = ((s8[6291456]{0:T(1024)(128)(4,1)}), s8[2097152]{0:T(1024)(128)(4,1)S(1)}, s32[]{:S(2)}) async-start(s8[6291456]{0:T(1024)(128)(4,1)} %bitcast.157), calls=%async_computation.18 | async-start | bytes 4194304
  320.2 1.6 copy-start.4
  320.2 1.6 copy-start.7
  320.2 1.6 copy-start.10
  320.2 1.5 copy-start.14
  321.0 0.8 copy-start.16
  357.6 18.0 %all-to-all-start.11 = ((f32[8,128,256]{2,1,0:T(8,128)}), f32[8,128,256]{2,1,0:T(8,128)S(1)}, u32[]{:S(2)}, u32[]{:S(2)}) async-start(f32[8,128,256]{2,1,0:T(8,128)} %broadcast_in_dim.25), calls=%async_computation.11 | async-start | bytes 2097152 | tf_op jit(solution)/shard_map/all_to_all | solution.py:47
  375.7 15.6 %slice-start.4 = ((s8[6291456]{0:T(1024)(128)(4,1)}), s8[4194304]{0:T(1024)(128)(4,1)S(1)}, s32[]{:S(2)}) async-start(s8[6291456]{0:T(1024)(128)(4,1)} %bitcast.159), calls=%async_computation.19 | async-start | bytes 8388608
  375.9 15.1 %copy-start = (bf16[1,16,128,256]{3,2,1,0:T(8,128)(2,1)S(1)}, bf16[1,16,128,256]{3,2,1,0:T(8,128)(2,1)}, u32[]{:S(2)}) copy-start(bf16[1,16,128,256]{3,2,1,0:T(8,128)(2,1)} %get-tuple-element.15) | copy-start | bytes 3145732
  375.9 15.4 %slice-start.5 = ((s8[6291456]{0:T(1024)(128)(4,1)}), s8[2097152]{0:T(1024)(128)(4,1)S(1)}, s32[]{:S(2)}) async-start(s8[6291456]{0:T(1024)(128)(4,1)} %bitcast.159), calls=%async_computation.20 | async-start | bytes 4194304
  391.0 1.0 copy-start.5
  391.0 1.2 copy-start.8
  391.0 1.4 copy-start.11
  391.0 1.5 copy-start.15
  391.0 1.7 copy-start.17
  397.8 72.6 %all-to-all-start.13 = ((f32[4,512,256]{2,1,0:T(8,128)}), f32[4,512,256]{2,1,0:T(8,128)S(1)}, u32[]{:S(2)}, u32[]{:S(2)}) async-start(f32[4,512,256]{2,1,0:T(8,128)} %broadcast_in_dim.27), calls=%async_computation.13 | async-start | bytes 4194304 | tf_op jit(solution)/shard_map/all_to_all | solution.py:47
Sparse Core Ops, SparseCore 0:
  9.8 71.9 all-gather.2
